TPU v7x, 512 devices: a whole 4x4x16 slice. The times are simulated.
512 devices in a mesh: rows: 128 (over y, z, core), users: 4 (over x).
Axes of the slice: x: 4, y: 4, z: 16, core: 2. Of those that a mesh axis runs over, the one named last changes fastest.
Arguments:
- old_basis: bfloat16 [49152, 4096], P('rows', 'users'), may hold values from -24 to 24
- new_atoms: bfloat16 [49152, 128], P('rows'), may hold values from -300 to 300
- user_residuals: bfloat16 [49152, 512], P('rows', 'users'), may hold values from -850 to 850
Outputs:
- new_block: bfloat16 [49152, 128], P('rows')
- updated_residuals: bfloat16 [49152, 512], P('rows', 'users')
All inputs are finite; a program needn't handle non-finite values.
Results may differ from a plain program's by a relative error of at most 0.019.
Values may be sent and summed in bfloat16 or wider, within the bound.
A program may use at most 64 MiB of HBM per device.

v0:
```python
import jax
import jax.numpy as jnp
from jax import lax
from jax.sharding import PartitionSpec as P


def coefficient_sum(partial_coef, m_total):
    summed = lax.psum(partial_coef, "rows")
    return (summed / m_total).astype(jnp.bfloat16)


def rows_product(left_rows, right_rows):
    return jnp.einsum("rk,rb->kb", left_rows, right_rows, preferred_element_type=jnp.float32)


def finish_block(remainder_low, gram_total, coupling_total, user_residuals, m_total):
    gram_matrix = gram_total / m_total
    factor_lower = jnp.linalg.cholesky(gram_matrix)
    identity = jnp.eye(gram_matrix.shape[0], dtype=jnp.float32)
    inverse = jax.scipy.linalg.solve_triangular(factor_lower, identity, lower=True)
    new_block = jnp.dot(
        remainder_low.astype(jnp.float32), inverse.T, precision=lax.Precision.HIGHEST
    ).astype(jnp.bfloat16)
    weights_low = jnp.dot(
        inverse, coupling_total / m_total, precision=lax.Precision.HIGHEST
    ).astype(jnp.bfloat16)
    updated = user_residuals.astype(jnp.float32) - jnp.dot(
        new_block, weights_low, preferred_element_type=jnp.float32
    )
    return (new_block, updated.astype(jnp.bfloat16))


def local(old_basis, new_atoms, user_residuals):
    local_rows = old_basis.shape[0]
    m_total = float(local_rows * lax.axis_size("rows"))
    remainder = new_atoms.astype(jnp.float32)
    remainder_low = new_atoms
    for sweep_index in range(2):
        coef_low = coefficient_sum(rows_product(old_basis, remainder_low), m_total)
        local_image = jnp.dot(old_basis, coef_low, preferred_element_type=jnp.float32)
        projected = lax.psum(local_image, "users")
        remainder = remainder - projected
        remainder_low = remainder.astype(jnp.bfloat16)
    gram_total, coupling_total = lax.psum(
        (rows_product(remainder_low, remainder_low), rows_product(remainder_low, user_residuals)),
        "rows",
    )
    return finish_block(remainder_low, gram_total, coupling_total, user_residuals, m_total)


def solution(mesh):
    in_specs = (P("rows", "users"), P("rows", None), P("rows", "users"))
    out_specs = (P("rows", None), P("rows", "users"))
    return jax.shard_map(local, mesh=mesh, in_specs=in_specs, out_specs=out_specs, check_vma=False)
```

profile of v0, /device:TPU:2, one launch (start us, length us, event | category | flops | bytes accessed | tf_op | source)
XLA Modules:
  0.0 1168.0 jit_solution(7656072023004440981)
XLA Ops:
  7.2 0.0 copy-start
  7.2 0.0 all-reduce.7.cloned.1.call-start
  7.2 1.1 copy-done
  8.3 2.1 fusion.14
  10.4 0.0 all-reduce.7.cloned.1.call-update
  10.4 0.0 all-reduce.9.cloned.1.call-start
  10.5 341.6 %all-reduce.7.cloned.1.call-done = f32[1024,128]{1,0:T(8,128)} async-done(((f32[1024,128]{1,0:T(8,128)}), f32[1024,128]{1,0:T(8,128)}) %all-reduce.7.cloned.1.call-update) | async-done | bytes 524304 | tf_op jit(solution)/shard_map/psum | solution.py:8
  352.1 2.1 convolution_bitcast_fusion.2
  354.2 0.0 copy-start.4
  354.2 0.0 all-reduce.9.cloned.1.call-update
  354.2 0.0 all-reduce.11.cloned.1.call-start
  354.2 0.8 copy-done.4
  355.0 0.1 copy.5
  355.2 52.1 %all-reduce.9.cloned.1.call-done = f32[384,128]{0,1:T(8,128)} async-done(((f32[384,128]{0,1:T(8,128)}), f32[384,128]{0,1:T(8,128)}) %all-reduce.9.cloned.1.call-update) | async-done | bytes 196624 | tf_op jit(solution)/shard_map/psum | solution.py:41
  407.3 2.2 convolution_bitcast_fusion
  409.5 0.0 all-reduce.11.cloned.1.call-update
  409.5 0.0 all-reduce.13.cloned.1.call-start
  409.5 338.9 %all-reduce.11.cloned.1.call-done = f32[1024,128]{1,0:T(8,128)} async-done(((f32[1024,128]{1,0:T(8,128)}), f32[1024,128]{1,0:T(8,128)}) %all-reduce.11.cloned.1.call-update) | async-done | bytes 524304 | tf_op jit(solution)/shard_map/psum | solution.py:8
  748.4 2.1 convolution_bitcast_fusion.1
  750.5 0.0 copy-start.1
  750.5 0.0 all-reduce.13.cloned.1.call-update
  750.5 0.0 all-reduce.15.cloned.1.call-start
  750.6 53.0 %all-reduce.13.cloned.1.call-done = f32[384,128]{0,1:T(8,128)} async-done(((f32[384,128]{0,1:T(8,128)}), f32[384,128]{0,1:T(8,128)}) %all-reduce.13.cloned.1.call-update) | async-done | bytes 196624 | tf_op jit(solution)/shard_map/psum | solution.py:41
  803.6 0.0 copy-done.1
  803.6 1.0 subtract_convert_fusion
  804.5 0.0 copy-start.2
  804.5 0.8 fusion.15
  805.3 0.1 copy-done.2
  805.4 0.9 fusion.16
  806.3 0.0 all-reduce.15.cloned.1.call-update
  806.3 328.4 %all-reduce.15.cloned.1.call-done = (f32[128,128]{0,1:T(8,128)}, f32[128,128]{0,1:T(8,128)}) async-done(((f32[128,128]{0,1:T(8,128)}, f32[128,128]{0,1:T(8,128)}), (f32[128,128]{0,1:T(8,128)}, f32[128,128]{0,1:T(8,128)})) %all-reduce.15.cloned.1.call-update) | async-done | bytes 131088 | tf_op jit(solution)/shard_map/psum | solution.py:44
  1134.7 0.8 broadcast_multiply_fusion
  1135.5 0.0 copy-start.5
  1135.5 0.1 copy.7
  1135.6 0.7 copy-done.5
  1136.4 11.7 %cholesky.17 = f32[128,128]{1,0:T(8,128)S(1)} custom-call(f32[128,128]{1,0:T(8,128)S(1)} %fusion.8), custom_call_target="Cholesky" | custom-call | tf_op jit(solution)/shard_map/jit(cholesky)/cholesky | solution.py:18
  1148.1 0.6 compare_reduce_fusion
  1148.8 0.7 fusion.5
  1149.4 9.8 custom-call.7
  1159.3 0.2 fusion.6
  1159.5 0.0 copy-start.6
  1159.5 0.3 convolution_convert_fusion
  1159.8 0.0 copy-start.3
  1159.8 0.5 copy-done.6
  1160.4 0.3 convolution_convert_fusion.1
  1160.6 0.8 fusion
  1161.4 0.0 copy-done.3
  (2 shorter events, 0.0 us)
Async XLA Ops:
  7.2 1.1 copy-start
  7.2 344.9 %all-reduce.7.cloned.1.call-start = ((), (), s32[]{:S(2)}) async-start(), calls=%async_computation | async-start | bytes 1048576 | tf_op jit(solution)/shard_map/psum | solution.py:8
  10.4 396.9 %all-reduce.9.cloned.1.call-start = ((), (), s32[]{:S(2)}) async-start(), calls=%async_computation.1 | async-start | bytes 393216 | tf_op jit(solution)/shard_map/psum | solution.py:41
  354.2 0.9 copy-start.4
  354.2 394.2 %all-reduce.11.cloned.1.call-start = ((), (), s32[]{:S(2)}) async-start(), calls=%async_computation.2 | async-start | bytes 1048576 | tf_op jit(solution)/shard_map/psum | solution.py:8
  409.5 394.1 %all-reduce.13.cloned.1.call-start = ((), (), s32[]{:S(2)}) async-start(), calls=%async_computation.3 | async-start | bytes 393216 | tf_op jit(solution)/shard_map/psum | solution.py:41
  750.5 53.1 %copy-start.1 = (f32[384,128]{0,1:T(8,128)S(1)}, f32[384,128]{0,1:T(8,128)}, u32[]{:S(2)}) copy-start(f32[384,128]{0,1:T(8,128)} %all-reduce.9.cloned.1.call-done) | copy-start | bytes 589828
  750.5 384.2 %all-reduce.15.cloned.1.call-start = ((), (), s32[]{:S(2)}) async-start(), calls=%async_computation.4 | async-start | bytes 262144 | tf_op jit(solution)/shard_map/psum | solution.py:44
  804.5 0.9 copy-start.2
  1135.5 0.8 copy-start.5
  1159.5 0.8 copy-start.6
  1159.8 1.6 copy-start.3
Sparse Core Ops, SparseCore 0:
  11.4 340.5 all-reduce.6
  354.4 52.8 all-reduce.8
  410.7 337.6 all-reduce.10
  750.6 52.8 all-reduce.12
  807.5 327.1 all-reduce.14
where the time goes:
time: 1170 us
  waiting for transfers between devices  1110 us (95%)
  other arithmetic  24.7 us (2%)
  between operations  13.9 us (1%)
    psum x2, waiting for transfers between devices, coefficient_sum(): summed = lax.psum(partial_coef, 'rows')  680 us
    psum x1, waiting for transfers between devices, local(): lax.psum((rows_product(remainder_low, remainder_low), rows_product(remain...  328 us
    psum x2, waiting for transfers between devices, local(): projected = lax.psum(local_image, 'users')  105 us
  transfers between devices with their start and end apart: 5, of which 5 were waited for; matrix products, arithmetic and copies ran while one was open for 0% of the time, Pallas kernels for 0%

commit v1 on v0

--- a/solution.py
+++ b/solution.py
@@ -2,6 +2,12 @@
 import jax.numpy as jnp
 from jax import lax
 from jax.sharding import PartitionSpec as P
+
+
+def gather_and_add(value, mesh_axis):
+    shards = lax.all_gather(value, mesh_axis, axis=0, tiled=False)
+    total = shards.sum(axis=0)
+    return total
 
 
 def coefficient_sum(partial_coef, m_total):
@@ -38,7 +44,7 @@
     for sweep_index in range(2):
         coef_low = coefficient_sum(rows_product(old_basis, remainder_low), m_total)
         local_image = jnp.dot(old_basis, coef_low, preferred_element_type=jnp.float32)
-        projected = lax.psum(local_image, "users")
+        projected = gather_and_add(local_image, "users")
         remainder = remainder - projected
         remainder_low = remainder.astype(jnp.bfloat16)
     gram_total, coupling_total = lax.psum(

time: 1170 us -> 1080 us (0.923)
  waiting for transfers between devices: 1110 us -> 995 us
  blocking collectives: 0 us -> 28 us
    psum x2 -> x0, waiting for transfers between devices: 105 us -> none  [local(): projected = lax.psum(local_image, 'users')]
    all_gather x0 -> x2, blocking collectives: none -> 28 us  [gather_and_add(): shards = lax.all_gather(value, mesh_axis, axis=0, tiled=False)]
  transfers between devices with their start and end apart: 5 -> 3, of which waited for: 5 -> 3; matrix products, arithmetic and copies ran while one was open for 0% -> 0% of each run, Pallas kernels for 0% -> 0%
where the time goes in v1:
time: 1080 us
  waiting for transfers between devices  995 us (92%)
  blocking collectives  28 us (3%)
  other arithmetic  24.7 us (2%)
  between operations  13.9 us (1%)
    psum x2, waiting for transfers between devices, coefficient_sum(): summed = lax.psum(partial_coef, 'rows')  673 us
    psum x1, waiting for transfers between devices, local(): lax.psum((rows_product(remainder_low, remainder_low), rows_product(remain...  322 us
    all_gather x2, blocking collectives, gather_and_add(): shards = lax.all_gather(value, mesh_axis, axis=0, tiled=False)  28 us
  transfers between devices with their start and end apart: 3, of which 3 were waited for; matrix products, arithmetic and copies ran while one was open for 0% of the time, Pallas kernels for 0%

profile of v1, /device:TPU:2, one launch (start us, length us, event | category | flops | bytes accessed | tf_op | source)
XLA Modules:
  0.0 1075.5 jit_solution(16269930076162726520)
XLA Ops:
  7.2 0.0 copy-start
  7.2 0.0 all-reduce.5.cloned.1.call-start
  7.2 1.1 copy-done
  8.3 2.1 fusion.14
  10.4 0.0 copy-start.3
  10.4 0.0 all-reduce.5.cloned.1.call-update
  10.4 0.0 all-reduce.7.cloned.1.call-start
  10.5 0.8 copy-done.3
  11.3 0.1 copy.7
  11.4 340.5 %all-reduce.5.cloned.1.call-done = f32[1024,128]{1,0:T(8,128)} async-done(((f32[1024,128]{1,0:T(8,128)}), f32[1024,128]{1,0:T(8,128)}) %all-reduce.5.cloned.1.call-update) | async-done | bytes 524304 | tf_op jit(solution)/shard_map/psum | solution.py:14
  351.9 1.4 convolution_bitcast_fusion.2
  353.3 14.0 %all-gather = f32[1536,128]{0,1:T(8,128)S(1)} all-gather(f32[384,128]{0,1:T(8,128)S(1)} %convolution_bitcast_fusion.2), channel_id=2, replica_groups=mesh['rows'=128,'users'=4] {'users'}, dimensions={0}, use_global_device_ids=true | all-gather | bytes 983040 | tf_op jit(solution)/shard_map/all_gather | solution.py:8
  367.3 0.3 reshape.14
  367.6 0.5 reduce_sum.18
  368.1 1.3 convolution_bitcast_fusion
  369.3 0.0 all-reduce.7.cloned.1.call-update
  369.4 0.0 all-reduce.9.cloned.1.call-start
  369.4 332.3 %all-reduce.7.cloned.1.call-done = f32[1024,128]{1,0:T(8,128)} async-done(((f32[1024,128]{1,0:T(8,128)}), f32[1024,128]{1,0:T(8,128)}) %all-reduce.7.cloned.1.call-update) | async-done | bytes 524304 | tf_op jit(solution)/shard_map/psum | solution.py:14
  701.8 1.4 convolution_bitcast_fusion.1
  703.2 14.0 %all-gather.1 = f32[1536,128]{0,1:T(8,128)S(1)} all-gather(f32[384,128]{0,1:T(8,128)S(1)} %convolution_bitcast_fusion.1), channel_id=3, replica_groups=mesh['rows'=128,'users'=4] {'users'}, dimensions={0}, use_global_device_ids=true | all-gather | bytes 983040 | tf_op jit(solution)/shard_map/all_gather | solution.py:8
  717.2 0.3 reshape.15
  717.4 0.5 reduce_sum.19
  718.0 0.0 copy-start.1
  718.0 0.8 fusion.15
  718.8 0.1 copy-done.1
  718.9 0.9 fusion.16
  719.7 0.0 all-reduce.9.cloned.1.call-update
  719.7 322.5 %all-reduce.9.cloned.1.call-done = (f32[128,128]{0,1:T(8,128)}, f32[128,128]{0,1:T(8,128)}) async-done(((f32[128,128]{0,1:T(8,128)}, f32[128,128]{0,1:T(8,128)}), (f32[128,128]{0,1:T(8,128)}, f32[128,128]{0,1:T(8,128)})) %all-reduce.9.cloned.1.call-update) | async-done | bytes 131088 | tf_op jit(solution)/shard_map/psum | solution.py:50
  1042.2 0.8 broadcast_multiply_fusion
  1043.1 0.0 copy-start.4
  1043.1 0.1 copy.9
  1043.2 0.7 copy-done.4
  1043.9 11.7 %cholesky.17 = f32[128,128]{1,0:T(8,128)S(1)} custom-call(f32[128,128]{1,0:T(8,128)S(1)} %fusion.8), custom_call_target="Cholesky" | custom-call | tf_op jit(solution)/shard_map/jit(cholesky)/cholesky | solution.py:24
  1055.7 0.6 compare_reduce_fusion
  1056.3 0.7 fusion.5
  1057.0 9.8 custom-call.7
  1066.8 0.2 fusion.6
  1067.0 0.0 copy-start.5
  1067.0 0.3 convolution_convert_fusion
  1067.3 0.0 copy-start.2
  1067.4 0.5 copy-done.5
  1067.9 0.3 convolution_convert_fusion.1
  1068.1 0.8 fusion
  1069.0 0.0 copy-done.2
  (3 shorter events, 0.1 us)
Async XLA Ops:
  7.2 1.1 copy-start
  7.2 344.7 %all-reduce.5.cloned.1.call-start = ((), (), s32[]{:S(2)}) async-start(), calls=%async_computation | async-start | bytes 1048576 | tf_op jit(solution)/shard_map/psum | solution.py:14
  10.4 0.9 copy-start.3
  10.4 691.3 %all-reduce.7.cloned.1.call-start = ((), (), s32[]{:S(2)}) async-start(), calls=%async_computation.1 | async-start | bytes 1048576 | tf_op jit(solution)/shard_map/psum | solution.py:14
  369.4 672.9 %all-reduce.9.cloned.1.call-start = ((), (), s32[]{:S(2)}) async-start(), calls=%async_computation.2 | async-start | bytes 262144 | tf_op jit(solution)/shard_map/psum | solution.py:50
  718.0 0.9 copy-start.1
  1043.1 0.8 copy-start.4
  1067.0 0.8 copy-start.5
  1067.3 1.6 copy-start.2
Sparse Core Ops, SparseCore 0:
  11.4 340.4 all-reduce.4
  369.5 332.2 all-reduce.6
  719.9 322.3 all-reduce.8
